TPU v7x, 32 devices: a whole 2x2x4 slice. The times are simulated.
32 devices in a mesh: lat: 8 (over z, y), rad: 4 (over x, core).
Axes of the slice: x: 2, y: 2, z: 4, core: 2. Of those that a mesh axis runs over, the one named last changes fastest.
Arguments:
- source: float32 [128, 32768], P('rad', 'lat'), may hold values from -6 to 6
- to_modes: float32 [128, 128], replicated, may hold values from -0.5 to 0.5
- from_modes: float32 [128, 128], replicated, may hold values from -0.5 to 0.5
- eigenvalue: float32 [128], replicated, may hold values from 0.1 to 20
- shifts: float32 [32768], P('lat'), may hold values from 0.5 to 2
- weights: float32 [31, 32768], P(None, 'lat'), may hold values from 0.02 to 0.12
- neighbors: int32 [31, 256], P(None, 'lat'), may hold values from -8 to 8, as said below
Outputs:
- smoothed: float32 [128, 32768], P('rad', 'lat')
- residual_norm: float32 [128], P('rad')
Inputs may be any that keep to these rules, and one draw needn't show every extreme that they name: `neighbors`: every entry is nonzero; some entry equals -8.
All inputs are finite; a program needn't handle non-finite values.
Results may differ from a plain program's by a relative error of at most 0.000073.
Values sent between devices are 32-bit elements; how exact they have to be, the bound alone decides.
A program may use at most 64 MiB of HBM per device.

v0:
```python
import jax
import jax.numpy as jnp
from jax import lax
from jax.sharding import PartitionSpec as P

BLOCK = 128
HALO_BLOCKS = 8


def extended_2(value, sides, width):
    for axis, dim in sides:
        devices, length = (lax.axis_size(axis), value.shape[dim])
        up = [(i, (i + 1) % devices) for i in range(devices)]
        down = [(j, i) for i, j in up]
        last = lax.slice_in_dim(value, length - width, length, axis=dim)
        initial = lax.slice_in_dim(value, 0, width, axis=dim)
        before = lax.ppermute(last, axis, up)
        after = lax.ppermute(initial, axis, down)
        value = jnp.concatenate([before, value, after], axis=dim)
    return value


def on_device(source, to_modes, from_modes, eigenvalue, shifts, weights, neighbors):
    slab = source.shape[0]
    node_count = source.shape[1]
    rad_index = lax.axis_index("rad")
    level_cols = lax.dynamic_slice_in_dim(to_modes, rad_index * slab, slab, 1)
    modal = lax.psum_scatter(
        jnp.dot(
            level_cols, source, precision=lax.Precision.HIGHEST, preferred_element_type=jnp.float32
        ),
        "rad",
        scatter_dimension=0,
        tiled=True,
    )
    eig_local = lax.dynamic_slice_in_dim(eigenvalue, rad_index * slab, slab)
    block_count = node_count // BLOCK
    ext_count = block_count + 2 * HALO_BLOCKS
    block_local = jnp.arange(block_count, dtype=jnp.int32)
    wanted = block_local[None, :] + HALO_BLOCKS + neighbors
    ext_ids = jnp.arange(ext_count, dtype=jnp.int32)
    selector = (wanted[:, :, None] == ext_ids[None, None, :]).astype(jnp.float32)
    total = jnp.sum(weights, axis=0)
    coeffs = (shifts + total)[None, :] + eig_local[:, None]
    slot_weights = weights.reshape(weights.shape[0], block_count, BLOCK)

    def operate(field):
        extended = extended_2(field, (("lat", 1),), HALO_BLOCKS * BLOCK)
        ext_blocks = extended.reshape(slab, ext_count, BLOCK)
        picked = jnp.einsum(
            "sjc,kcb->skjb",
            selector,
            ext_blocks,
            precision=lax.Precision.HIGHEST,
            preferred_element_type=jnp.float32,
        )
        coupled = jnp.zeros((slab, block_count, BLOCK), jnp.float32)
        for slot_index in range(weights.shape[0]):
            moved = jnp.roll(picked[slot_index], -(slot_index % BLOCK), axis=2)
            coupled = coupled + slot_weights[slot_index][None, :, :] * moved
        return coeffs * field - coupled.reshape(slab, node_count)

    image = operate(modal)
    base, power = lax.psum((jnp.sum(modal * modal, axis=1), jnp.sum(image * image, axis=1)), "lat")
    upper = 1.5 * jnp.sqrt(power / (base + 1e-06))
    lower = upper * 0.125
    center = ((upper + lower) * 0.5)[:, None]
    half_width = ((upper - lower) * 0.5)[:, None]
    sigma = center / half_width
    rho_zero = 1.0 / sigma
    rho_one = 1.0 / (2.0 * sigma - rho_zero)
    first = modal / center
    second_res = modal - image / center
    update = rho_one * rho_zero * first + 2.0 * rho_one / half_width * second_res
    iterate = first + update
    final_res = second_res - operate(update)
    squares = lax.psum(jnp.sum(final_res * final_res, axis=1), "lat")
    residual_norm = jnp.sqrt(squares / (base + 1e-06))
    level_rows = lax.dynamic_slice_in_dim(from_modes, rad_index * slab, slab, 0)
    smoothed = jnp.dot(
        level_rows,
        lax.all_gather(iterate, "rad", axis=0, tiled=True),
        precision=lax.Precision.HIGHEST,
        preferred_element_type=jnp.float32,
    )
    return (smoothed, residual_norm)


def solution(mesh):
    return jax.shard_map(
        on_device,
        mesh=mesh,
        in_specs=(P("rad", "lat"), P(), P(), P(), P("lat"), P(None, "lat"), P(None, "lat")),
        out_specs=(P("rad", "lat"), P("rad")),
        check_vma=False,
    )
```

profile of v0, /device:TPU:0, one launch (start us, length us, event | category | flops | bytes accessed | tf_op | source)
XLA Modules:
  0.0 221.5 jit_solution(6774470598374039520)
XLA Ops:
  8.2 4.0 %fusion.73 = f32[128,4096]{1,0:T(8,128)} fusion(f32[32,4096]{1,0:T(8,128)S(1)} %copy-done, f32[128,128]{1,0:T(8,128)} %param.8, s32[]{:T(128)S(6)} %select_n.2), kind=kOutput, calls=%fused_computation.265 | convolution fusion | flops 201326592 | bytes 2686980 | tf_op jit(solution)/shard_map/dot_general | solution.py:29
  13.0 1.1 reduce_sum.36
  15.6 1.7 fusion.86
  17.3 3.3 %fusion.85 = (f32[1,4096]{1,0:T(1,128)S(1)}, f32[1,4096]{1,0:T(1,128)S(1)}, f32[1,4096]{1,0:T(1,128)S(1)}, f32[1,4096]{1,0:T(1,128)S(1)}, f32[1,4096]{1,0:T(1,12...) fusion(f32[31,4096]{1,0:T(8,128)} %param.12), kind=kLoop, calls=%fused_computation.284 | loop fusion | bytes 622592 | tf_op jit(solution)/shard_map/slice | solution.py:60
  20.7 25.6 %reduce-scatter.2.cloned.1.call-done = f32[32,4096]{1,0:T(8,128)} async-done(((f32[128,4096]{1,0:T(8,128)}), f32[32,4096]{1,0:T(8,128)}) %reduce-scatter.2.cloned.1.call-update) | async-done | bytes 524304 | tf_op jit(solution)/shard_map/reduce_scatter | solution.py:28
  46.3 1.0 fusion.87
  47.3 1.5 collective-permute-start
  48.8 3.4 %collective-permute-start.1 = (f32[32,1024]{1,0:T(8,128)S(1)}, f32[32,1024]{1,0:T(8,128)S(1)}, u32[]{:S(2)}, u32[]{:S(2)}) collective-permute-start(f32[32,1024]{1,0:T(8,128)S(1)} %get-tuple-element.109), channel_id=1, source_target_pairs={{4,0},{8,4},{12,8},{16,12},{20,16},{24,20},{28,24},{0,28},{5,1},{9... | collective-permute-start | bytes 393224 | tf_op jit(solution)/shard_map/ppermute | solution.py:18
  52.2 1.2 multiply_reduce_fusion
  53.4 1.8 collective-permute-done
  55.2 1.4 collective-permute-done.1
  56.6 1.1 maximum_bitcast_fusion
  57.8 6.6 %convolution_bitcast_fusion.1 = f32[31,32,32,128]{3,2,0,1:T(8,128)S(1)} fusion(f32[32,48,128,1]{2,1,0,3:T(8,128)S(1)} %bitcast.754, s32[31,32]{1,0:T(8,128)S(1)} %broadcast_add_fusion), kind=kOutput, calls=%fused_computation.1 | convolution fusion | flops 2340469248 | bytes 17043328 | tf_op jit(solution)/shard_map/sjc,kcb->skjb/dot_general | solution.py:50
  64.4 5.6 %copy-done.3 = f32[31,32,32,128]{3,2,0,1:T(8,128)} copy-done((f32[31,32,32,128]{3,2,0,1:T(8,128)}, f32[31,32,32,128]{3,2,0,1:T(8,128)S(1)}, u32[]{:S(2)}) %copy-start.3) | copy-done | bytes 16252952
  70.0 1.5 fusion.83
  71.5 5.1 %slice_bitcast_fusion.55 = (f32[32,32,128]{2,1,0:T(8,128)S(1)}, f32[32,32,128]{2,1,0:T(8,128)S(1)}, f32[32,32,128]{2,1,0:T(8,128)S(1)}, f32[32,32,128]{2,1,0:T(8...) fusion(f32[31,32,32,128]{3,2,0,1:T(8,128)} %copy-done.3), kind=kLoop, calls=%fused_computation.190 | loop fusion | bytes 19922944 | tf_op jit(solution)/shard_map/squeeze | solution.py:59
  90.5 2.3 %fusion.63 = f32[32,4096]{1,0:T(8,128)S(1)} fusion(f32[4,8,32,128]{3,2,1,0:T(8,128)S(1)} %bitcast.794, f32[4,8,32,128]{3,2,1,0:T(8,128)S(1)} %bitcast.796, f32[4,8,32,128]{3,2,1,0:T(8,128)S(1)} %bitcast.798, f32[4,8,32,128]{3,2,1,0:T(8,128)S(1)} %bitcast.800, f32[4,8,32,128]{3,2,1,0:T(8,128)S(1)} %bitcast.756, f32[4096]{0:T(1024)S(1)} %bitcast.821, ...), kind=kLoop, calls=%fused_computation.127 | loop fusion | flops 1179648 | bytes 3227648 | tf_op jit(solution)/shard_map/add | solution.py:60
  92.9 13.6 %multiply_reduce_fusion.1 = (f32[32]{0:T(128)S(1)}, f32[32,4096]{1,0:T(8,128)S(1)}) fusion(f32[4,8,32,128]{3,2,1,0:T(8,128)S(1)} %bitcast.787, f32[4096]{0:T(1024)S(1)} %bitcast.839, f32[4,8,32,128]{3,2,1,0:T(8,128)S(1)} %bitcast.790, f32[4096]{0:T(1024)S(1)} %bitcast.841, f32[4,8,32,128]{3,2,1,0:T(8,128)S(1)} %bitcast.793, f32[4096]{0:T(1024)S(1)} %bitcast.843, ...), kind=kLoop, calls=%fused_computation.258 | loop fusion | flops 7471072 | bytes 15646976 | tf_op jit(solution)/shard_map/reduce_sum | solution.py:64
  106.4 20.5 %all-reduce = (f32[32]{0:T(128)S(1)}, f32[32]{0:T(128)S(1)}) all-reduce(f32[32]{0:T(128)S(1)} %get-tuple-element.11, f32[32]{0:T(128)S(1)} %multiply_reduce_fusion), channel_id=1, replica_groups=mesh['lat'=8,'rad'=4] {'lat'}, use_global_device_ids=true, to_apply=%region_3.4 | all-reduce | flops 64 | bytes 512 | tf_op jit(solution)/shard_map/psum | solution.py:64
  127.6 1.2 fusion.72
  128.8 4.9 %collective-permute-start.3 = (f32[32,1024]{1,0:T(8,128)S(1)}, f32[32,1024]{1,0:T(8,128)S(1)}, u32[]{:S(2)}, u32[]{:S(2)}) collective-permute-start(f32[32,1024]{1,0:T(8,128)S(1)} %get-tuple-element.76), channel_id=1, source_target_pairs={{4,0},{8,4},{12,8},{16,12},{20,16},{24,20},{28,24},{0,28},{5,1},{9... | collective-permute-start | bytes 393224 | tf_op jit(solution)/shard_map/ppermute | solution.py:18
  133.7 2.8 %collective-permute-done.2 = f32[32,1024]{1,0:T(8,128)S(1)} collective-permute-done((f32[32,1024]{1,0:T(8,128)S(1)}, f32[32,1024]{1,0:T(8,128)S(1)}, u32[]{:S(2)}, u32[]{:S(2)}) %collective-permute-start.2) | collective-permute-done | bytes 131104 | tf_op jit(solution)/shard_map/ppermute | solution.py:17
  136.7 6.6 %convolution_bitcast_fusion = f32[31,32,32,128]{3,2,0,1:T(8,128)S(1)} fusion(f32[32,48,128,1]{2,1,0,3:T(8,128)S(1)} %bitcast.753, s32[31,32]{1,0:T(8,128)S(1)} %broadcast_add_fusion), kind=kOutput, calls=%fused_computation | convolution fusion | flops 2340469248 | bytes 17043328 | tf_op jit(solution)/shard_map/sjc,kcb->skjb/dot_general | solution.py:50
  143.3 5.6 %copy-done.2 = f32[31,32,32,128]{3,2,0,1:T(8,128)} copy-done((f32[31,32,32,128]{3,2,0,1:T(8,128)}, f32[31,32,32,128]{3,2,0,1:T(8,128)S(1)}, u32[]{:S(2)}) %copy-start.2) | copy-done | bytes 16252952
  148.8 1.5 fusion.82
  150.4 6.0 %slice_bitcast_fusion.23 = (f32[32,32,128]{2,1,0:T(8,128)}, f32[32,32,128]{2,1,0:T(8,128)S(1)}, f32[32,32,128]{2,1,0:T(8,128)S(1)}, f32[32,32,128]{2,1,0:T(8,128...) fusion(f32[31,32,32,128]{3,2,0,1:T(8,128)} %copy-done.2), kind=kLoop, calls=%fused_computation.158 | loop fusion | bytes 19922944 | tf_op jit(solution)/shard_map/squeeze | solution.py:59
  158.6 1.2 slice.1105
  159.8 1.2 pad_maximum_fusion.36
  171.5 3.4 %fusion.31 = f32[32,4096]{1,0:T(8,128)S(1)} fusion(f32[4,8,32,128]{3,2,1,0:T(8,128)S(1)} %bitcast.779, f32[4,8,32,128]{3,2,1,0:T(8,128)S(1)} %bitcast.781, f32[4,8,32,128]{3,2,1,0:T(8,128)S(1)} %bitcast.783, f32[4,8,32,128]{3,2,1,0:T(8,128)S(1)} %bitcast.785, f32[4,8,32,128]{3,2,1,0:T(8,128)S(1)} %bitcast.788, f32[4,8,32,128]{3,2,1,0:T(8,128)S(1)} %bitcast.791, ...), kind=kLoop, calls=%fused_computation.62 | loop fusion | flops 1703936 | bytes 4308992 | tf_op jit(solution)/shard_map/add | solution.py:60
  174.9 13.4 %fusion.6 = f32[32]{0:T(128)S(1)} fusion(f32[32,4096]{1,0:T(8,128)S(1)} %copy-done.7, f32[32,4096]{1,0:T(8,128)S(1)} %get-tuple-element.5, f32[4,8,32,128]{3,2,1,0:T(8,128)S(1)} %bitcast.762, f32[4,8,32,128]{3,2,1,0:T(8,128)S(1)} %bitcast.763, f32[4,8,32,128]{3,2,1,0:T(8,128)S(1)} %bitcast.764, f32[4,8,32,128]{3,2,1,0:T(8,128)S(1)} %bitcast.765, ...), kind=kLoop, calls=%fused_computation.12 | loop fusion | flops 7077856 | bytes 14565632 | tf_op jit(solution)/shard_map/reduce_sum | solution.py:77
  188.3 22.0 %psum.23 = f32[32]{0:T(128)S(1)} all-reduce(f32[32]{0:T(128)S(1)} %fusion.6), channel_id=1, replica_groups=mesh['lat'=8,'rad'=4] {'lat'}, use_global_device_ids=true, to_apply=%region_7.8 | all-reduce | flops 32 | bytes 256 | tf_op jit(solution)/shard_map/psum | solution.py:77
  210.8 3.6 %fusion.75 = f32[32,4096]{1,0:T(8,128)} fusion(f32[128,4096]{1,0:T(8,128)} %all-gather.2.cloned.1.call-done, f32[128,128]{1,0:T(8,128)} %param.9, s32[]{:T(128)S(6)} %select_n.2), kind=kOutput, calls=%fused_computation.267 | convolution fusion | flops 201326592 | bytes 2637828 | tf_op jit(solution)/shard_map/dot_general | solution.py:80
  (191 shorter events, 30.9 us)
Async XLA Ops:
  7.2 1.1 copy-start
  7.2 39.1 %reduce-scatter.2.cloned.1.call-start = ((), (), s32[]{:S(2)}) async-start(), calls=%async_computation.1 | async-start | bytes 2621440 | tf_op jit(solution)/shard_map/reduce_scatter | solution.py:28
  12.3 198.6 %all-gather.2.cloned.1.call-start = ((), (), s32[]{:S(2)}) async-start(), calls=%async_computation.2 | async-start | bytes 2621440 | tf_op jit(solution)/shard_map/all_gather | solution.py:82
  13.0 79.8 %copy-start.22 = (f32[32]{0:T(128)}, f32[32]{0:T(128)S(1)}, u32[]{:S(2)}) copy-start(f32[32]{0:T(128)S(1)} %dynamic_slice.11) | copy-start | bytes 388
  20.6 72.2 %copy-start.8 = (f32[1,4096]{1,0:T(1,128)}, f32[1,4096]{1,0:T(1,128)S(1)}, u32[]{:S(2)}) copy-start(f32[1,4096]{1,0:T(1,128)S(1)} %get-tuple-element.89) | copy-start | bytes 49156
  20.6 72.2 %copy-start.10 = (f32[1,4096]{1,0:T(1,128)}, f32[1,4096]{1,0:T(1,128)S(1)}, u32[]{:S(2)}) copy-start(f32[1,4096]{1,0:T(1,128)S(1)} %get-tuple-element.90) | copy-start | bytes 49156
  20.6 72.2 %copy-start.12 = (f32[1,4096]{1,0:T(1,128)}, f32[1,4096]{1,0:T(1,128)S(1)}, u32[]{:S(2)}) copy-start(f32[1,4096]{1,0:T(1,128)S(1)} %get-tuple-element.91) | copy-start | bytes 49156
  20.6 72.2 %copy-start.14 = (f32[1,4096]{1,0:T(1,128)}, f32[1,4096]{1,0:T(1,128)S(1)}, u32[]{:S(2)}) copy-start(f32[1,4096]{1,0:T(1,128)S(1)} %get-tuple-element.92) | copy-start | bytes 49156
  20.6 72.2 %copy-start.16 = (f32[1,4096]{1,0:T(1,128)}, f32[1,4096]{1,0:T(1,128)S(1)}, u32[]{:S(2)}) copy-start(f32[1,4096]{1,0:T(1,128)S(1)} %get-tuple-element.93) | copy-start | bytes 49156
  47.3 7.9 %collective-permute-start = (f32[32,1024]{1,0:T(8,128)S(1)}, f32[32,1024]{1,0:T(8,128)S(1)}, u32[]{:S(2)}, u32[]{:S(2)}) collective-permute-start(f32[32,1024]{1,0:T(8,128)S(1)} %get-tuple-element.108), channel_id=1, source_target_pairs={{0,4},{4,8},{8,12},{12,16},{16,20},{20,24},{24,28},{28,0},{1,5},{5... | collective-permute-start | bytes 393224 | tf_op jit(solution)/shard_map/ppermute | solution.py:17
  48.8 7.8 %collective-permute-start.1 = (f32[32,1024]{1,0:T(8,128)S(1)}, f32[32,1024]{1,0:T(8,128)S(1)}, u32[]{:S(2)}, u32[]{:S(2)}) collective-permute-start(f32[32,1024]{1,0:T(8,128)S(1)} %get-tuple-element.109), channel_id=1, source_target_pairs={{4,0},{8,4},{12,8},{16,12},{20,16},{24,20},{28,24},{0,28},{5,1},{9... | collective-permute-start | bytes 393224 | tf_op jit(solution)/shard_map/ppermute | solution.py:18
  64.4 5.6 %copy-start.3 = (f32[31,32,32,128]{3,2,0,1:T(8,128)}, f32[31,32,32,128]{3,2,0,1:T(8,128)S(1)}, u32[]{:S(2)}) copy-start(f32[31,32,32,128]{3,2,0,1:T(8,128)S(1)} %convolution_bitcast_fusion.1) | copy-start | bytes 48758788
  86.0 4.5 %copy-start.6 = (f32[1,32,32,128]{3,2,0,1:T(8,128)S(1)}, f32[1,32,32,128]{3,2,0,1:T(8,128)}, u32[]{:S(2)}) copy-start(f32[1,32,32,128]{3,2,0,1:T(8,128)} %get-tuple-element.63) | copy-start | bytes 1572868
  86.7 6.2 %copy-start.4 = (f32[32,4096]{1,0:T(8,128)S(1)}, f32[32,4096]{1,0:T(8,128)}, u32[]{:S(2)}) copy-start(f32[32,4096]{1,0:T(8,128)} %reduce-scatter.2.cloned.1.call-done) | copy-start | bytes 1572868
  86.7 6.2 %copy-start.18 = (f32[1,4096]{1,0:T(1,128)S(1)}, f32[1,4096]{1,0:T(1,128)}, u32[]{:S(2)}) copy-start(f32[1,4096]{1,0:T(1,128)} %get-tuple-element.94) | copy-start | bytes 49156
  86.7 6.2 %copy-start.20 = (f32[1,4096]{1,0:T(1,128)S(1)}, f32[1,4096]{1,0:T(1,128)}, u32[]{:S(2)}) copy-start(f32[1,4096]{1,0:T(1,128)} %get-tuple-element.95) | copy-start | bytes 49156
  127.0 0.6 copy-start.24
  128.8 7.7 %collective-permute-start.2 = (f32[32,1024]{1,0:T(8,128)S(1)}, f32[32,1024]{1,0:T(8,128)S(1)}, u32[]{:S(2)}, u32[]{:S(2)}) collective-permute-start(f32[32,1024]{1,0:T(8,128)S(1)} %get-tuple-element.75), channel_id=1, source_target_pairs={{0,4},{4,8},{8,12},{12,16},{16,20},{20,24},{24,28},{28,0},{1,5},{5... | collective-permute-start | bytes 393224 | tf_op jit(solution)/shard_map/ppermute | solution.py:17
  128.8 7.7 %collective-permute-start.3 = (f32[32,1024]{1,0:T(8,128)S(1)}, f32[32,1024]{1,0:T(8,128)S(1)}, u32[]{:S(2)}, u32[]{:S(2)}) collective-permute-start(f32[32,1024]{1,0:T(8,128)S(1)} %get-tuple-element.76), channel_id=1, source_target_pairs={{4,0},{8,4},{12,8},{16,12},{20,16},{24,20},{28,24},{0,28},{5,1},{9... | collective-permute-start | bytes 393224 | tf_op jit(solution)/shard_map/ppermute | solution.py:18
  143.3 5.6 %copy-start.2 = (f32[31,32,32,128]{3,2,0,1:T(8,128)}, f32[31,32,32,128]{3,2,0,1:T(8,128)S(1)}, u32[]{:S(2)}) copy-start(f32[31,32,32,128]{3,2,0,1:T(8,128)S(1)} %convolution_bitcast_fusion) | copy-start | bytes 48758788
  166.9 4.5 %copy-start.5 = (f32[1,32,32,128]{3,2,0,1:T(8,128)S(1)}, f32[1,32,32,128]{3,2,0,1:T(8,128)}, u32[]{:S(2)}) copy-start(f32[1,32,32,128]{3,2,0,1:T(8,128)} %get-tuple-element.32) | copy-start | bytes 1572868
  167.6 7.3 %copy-start.7 = (f32[32,4096]{1,0:T(8,128)S(1)}, f32[32,4096]{1,0:T(8,128)}, u32[]{:S(2)}) copy-start(f32[32,4096]{1,0:T(8,128)} %get-tuple-element.6) | copy-start | bytes 1572868
  167.6 7.3 %copy-start.9 = (f32[1,4096]{1,0:T(1,128)S(1)}, f32[1,4096]{1,0:T(1,128)}, u32[]{:S(2)}) copy-start(f32[1,4096]{1,0:T(1,128)} %copy-done.8) | copy-start | bytes 49156
  167.6 7.3 %copy-start.11 = (f32[1,4096]{1,0:T(1,128)S(1)}, f32[1,4096]{1,0:T(1,128)}, u32[]{:S(2)}) copy-start(f32[1,4096]{1,0:T(1,128)} %copy-done.10) | copy-start | bytes 49156
  167.6 7.3 %copy-start.13 = (f32[1,4096]{1,0:T(1,128)S(1)}, f32[1,4096]{1,0:T(1,128)}, u32[]{:S(2)}) copy-start(f32[1,4096]{1,0:T(1,128)} %copy-done.12) | copy-start | bytes 49156
  167.6 7.3 %copy-start.15 = (f32[1,4096]{1,0:T(1,128)S(1)}, f32[1,4096]{1,0:T(1,128)}, u32[]{:S(2)}) copy-start(f32[1,4096]{1,0:T(1,128)} %copy-done.14) | copy-start | bytes 49156
  167.6 7.3 %copy-start.17 = (f32[1,4096]{1,0:T(1,128)S(1)}, f32[1,4096]{1,0:T(1,128)}, u32[]{:S(2)}) copy-start(f32[1,4096]{1,0:T(1,128)} %copy-done.16) | copy-start | bytes 49156
  167.6 7.3 %copy-start.19 = (f32[1,4096]{1,0:T(1,128)S(1)}, f32[1,4096]{1,0:T(1,128)}, u32[]{:S(2)}) copy-start(f32[1,4096]{1,0:T(1,128)} %get-tuple-element.94) | copy-start | bytes 49156
  167.6 7.3 %copy-start.21 = (f32[1,4096]{1,0:T(1,128)S(1)}, f32[1,4096]{1,0:T(1,128)}, u32[]{:S(2)}) copy-start(f32[1,4096]{1,0:T(1,128)} %get-tuple-element.95) | copy-start | bytes 49156
  167.7 7.3 %copy-start.23 = (f32[32]{0:T(128)S(1)}, f32[32]{0:T(128)}, u32[]{:S(2)}) copy-start(f32[32]{0:T(128)} %copy-done.22) | copy-start | bytes 388
  169.5 40.7 %copy-start.25 = (f32[32]{0:T(128)S(1)}, f32[32]{0:T(128)}, u32[]{:S(2)}) copy-start(f32[32]{0:T(128)} %copy-done.24) | copy-start | bytes 388
  170.0 44.4 %copy-start.1 = (f32[32,4096]{1,0:T(8,128)S(1)}, f32[32,4096]{1,0:T(8,128)}, u32[]{:S(2)}) copy-start(f32[32,4096]{1,0:T(8,128)} %param.7) | copy-start | bytes 1572868
Sparse Core Ops, SparseCore 0:
  12.4 33.8 reduce-scatter.1
  133.8 18.6 all-gather.1
where the time goes:
time: 225 us; the launch traced here: 222 us
  other arithmetic  53 us (24%)
  local copies, waits for them, and re-layouts  48.7 us (22%)
  blocking collectives  42.5 us (19%)
  waiting for transfers between devices  31.6 us (14%)
  matrix products  20.7 us (9%)
  between operations  15.1 us (7%)
  starting transfers between devices  9.93 us (4%)
    reduce_scatter x1, waiting for transfers between devices, on_device(): lax.psum_scatter(jnp.dot(level_cols, source, precision=lax.Precision.HIGH...  25.6 us
    psum x1, blocking collectives, on_device(): squares = lax.psum(jnp.sum(final_res * final_res, axis=1), 'lat')  22 us
    psum x1, blocking collectives, on_device(): lax.psum((jnp.sum(modal * modal, axis=1), jnp.sum(image * image, axis=1))...  20.5 us
    slice x62, local copies, waits for them, and re-layouts, operate(): moved = jnp.roll(picked[slot_index], -(slot_index % BLOCK), axis=2)  16.5 us
    unnamed x58, local copies, waits for them, and re-layouts  14.3 us
    concatenate x60, other arithmetic, operate(): moved = jnp.roll(picked[slot_index], -(slot_index % BLOCK), axis=2)  13.7 us
    reduce_sum x1, other arithmetic, on_device(): jnp.sum(image * image, axis=1)  13.6 us
    reduce_sum x1, other arithmetic, on_device(): squares = lax.psum(jnp.sum(final_res * final_res, axis=1), 'lat')  13.4 us
  transfers between devices with their start and end apart: 6, of which 4 were waited for; matrix products, arithmetic and copies ran while one was open for 25% of the time, Pallas kernels for 0%

commit v1 on v0

v1 whole, which is shorter than its diff:
```python
import functools

import jax
import jax.numpy as jnp
from jax import lax
from jax.experimental import pallas as pl
from jax.experimental.pallas import tpu as pltpu
from jax.sharding import PartitionSpec as P

BLOCK = 128
HALO = 8
CHUNKS = 4
GROUP = 8
CORES = 2
HIGHEST = lax.Precision.HIGHEST
MESH = pl.DeviceIdType.MESH


def dot(a, b):
    return jnp.dot(a, b, precision=HIGHEST, preferred_element_type=jnp.float32)


def kernel(
    L, R, S,
    src, w_hbm, to_ref, from_ref, eig_ref, shift_ref, nbr_ref,
    out, res_ref,
    gathered, wv, wr, ext1, ext2, modal, image, eig_t, coef, part, rows, s1, s2, s3, s4,
    own_sem, w_sem, ag_send, ag_recv, h1_send, h1_recv, h2_send, h2_recv, im_send, im_recv,
    s1_send, s1_recv, s2_send, s2_recv, s3_send, s3_recv, s4_send, s4_recv,
    out_send, out_recv, out_sem,
):
    T = CHUNKS
    X = R // CORES
    slab, nodes = src.shape
    K = slab * CORES
    half = nodes // CORES
    NB = half // BLOCK
    CB = NB // T
    CW = CB * BLOCK
    E = NB + 2 * HALO
    A = -(-S // GROUP)
    lat = lax.axis_index("lat")
    rad = lax.axis_index("rad")
    core = lax.rem(rad, CORES)
    chip = lax.div(rad, CORES)
    partner = chip * CORES + (1 - core)
    left_lat = lax.rem(lat + (L - 1) * (1 - core), L)
    right_lat = lax.rem(lat + core, L)

    def order(t, c):
        return t * (1 - c) + (T - 1 - t) * c

    def own_copy(q):
        return pltpu.make_async_copy(
            src.at[:, pl.ds(pl.multiple_of(core * half + q * CW, BLOCK), CW)],
            gathered.at[q, pl.ds(pl.multiple_of(rad * slab, 8), slab), :],
            own_sem.at[q],
        )

    w_copy = pltpu.make_async_copy(
        w_hbm.at[:, pl.ds(pl.multiple_of(core * half, BLOCK), half)], wv, w_sem
    )
    for q in range(T):
        own_copy(q).start()
    w_copy.start()

    barrier = pltpu.get_barrier_semaphore()
    for j in range(1, R):
        pl.semaphore_signal(
            barrier, inc=1, device_id={"lat": lat, "rad": lax.rem(rad + j, R)}, device_id_type=MESH
        )
    other_lat = left_lat * (1 - core) + right_lat * core
    pl.semaphore_signal(
        barrier, inc=1, device_id={"lat": other_lat, "rad": partner}, device_id_type=MESH
    )
    for j in range(1, L):
        pl.semaphore_signal(
            barrier, inc=1, device_id={"lat": lax.rem(lat + j, L), "rad": rad}, device_id_type=MESH
        )
    pl.semaphore_wait(barrier, R - 1 + 1 + L - 1)

    pending = []

    def remote(src_ref, dst_ref, send, recv, lat_to, rad_to):
        copy = pltpu.make_async_remote_copy(
            src_ref=src_ref, dst_ref=dst_ref, send_sem=send, recv_sem=recv,
            device_id={"lat": lat_to, "rad": rad_to}, device_id_type=MESH,
        )
        copy.start()
        pending.append(copy)

    def arrived(dst_ref, send, recv):
        pltpu.make_async_remote_copy(
            src_ref=dst_ref, dst_ref=dst_ref, send_sem=send, recv_sem=recv,
            device_id={"lat": lat, "rad": partner}, device_id_type=MESH,
        ).wait_recv()

    def slot(q, r):
        return gathered.at[q, pl.ds(pl.multiple_of(r * slab, 8), slab), :]

    for t in range(T):
        for j in range(1, R):
            to = lax.rem(rad + j, R)
            to_core = lax.rem(to, CORES)
            q = order(t, to_core)
            remote(
                src.at[:, pl.ds(pl.multiple_of(to_core * half + q * CW, BLOCK), CW)],
                slot(q, rad), ag_send.at[t, j - 1], ag_recv.at[q, rad], lat, to,
            )

    w_copy.wait()
    row_id = lax.broadcasted_iota(jnp.int32, (A * GROUP, BLOCK), 0)
    shift_rows = shift_ref[pl.ds(pl.multiple_of(core * NB, 8), NB), :]
    rows[...] = shift_rows

    def prepare(b, carry):
        wr[b, pl.ds((A - 1) * GROUP, GROUP), :] = jnp.zeros((GROUP, BLOCK), jnp.float32)
        wr[b, pl.ds(0, S), :] = wv[:, pl.ds(pl.multiple_of(b * BLOCK, BLOCK), BLOCK)]
        tile = wr[b, pl.ds(0, A * GROUP), :]
        placed = tile
        for c in range(1, GROUP):
            placed = jnp.where(lax.rem(row_id, GROUP) == c, pltpu.roll(tile, c, 1), placed)
        wr[b, pl.ds(0, A * GROUP), :] = placed
        diagonal = jnp.sum(tile, axis=0, keepdims=True) + rows[pl.ds(b, 1), :]
        wr[b, pl.ds(A * GROUP, GROUP), :] = jnp.broadcast_to(diagonal, (GROUP, BLOCK))
        return carry

    lax.fori_loop(0, NB, prepare, 0)
    levels = to_ref.shape[0]
    eig_t[...] = jnp.transpose(jnp.broadcast_to(eig_ref[...], (levels, levels)))
    eig = pl.ds(pl.multiple_of(chip * K, 8), K)

    def halo_send(buf, q, send, recv):
        upper = lax.div(q * 2, T)
        to_lat = left_lat * (1 - upper) + right_lat * upper
        at = HALO + q * CB
        dst = at + NB * (1 - upper) - NB * upper
        remote(
            buf.at[pl.ds(at, CB)], buf.at[pl.ds(dst, CB)], send.at[q], recv.at[q], to_lat, partner
        )

    def halo_wait(buf, send, recv):
        for q in range(T):
            dst = HALO + q * CB + (NB if q * 2 < T else -NB)
            arrived(buf.at[pl.ds(dst, CB)], send.at[q], recv.at[q])

    def spread(buf, k, value):
        for a in range(1, A):
            buf[a * E + k] = pltpu.roll(value, BLOCK - a * GROUP, 1)

    def spread_halo(buf):
        def step(k, carry):
            spread(buf, k, buf[k])
            spread(buf, k + NB + HALO, buf[k + NB + HALO])
            return carry

        lax.fori_loop(0, HALO, step, 0)

    own_rows = to_ref[pl.ds(pl.multiple_of(chip * K, 8), K), :]
    for t in range(T):
        q = order(t, core)
        own_copy(q).wait()
        for j in range(1, R):
            r = lax.rem(rad + j, R)
            arrived(slot(q, r), ag_send.at[t, j - 1], ag_recv.at[q, r])
        product = dot(own_rows, gathered[q])
        for i in range(CB):
            value = product[:, i * BLOCK:(i + 1) * BLOCK]
            ext1[HALO + q * CB + i] = value
            modal[chip, q * CB + i] = value
        halo_send(ext1, q, h1_send, h1_recv)
        for i in range(CB):
            spread(ext1, HALO + q * CB + i, product[:, i * BLOCK:(i + 1) * BLOCK])
    halo_wait(ext1, h1_send, h1_recv)
    spread_halo(ext1)

    def operate(buf, b, field):
        total = None
        for c in range(GROUP):
            inner = None
            for a in range(A):
                s = a * GROUP + c
                if s < S:
                    n = nbr_ref[s, core * NB + b]
                    term = buf[a * E + HALO + b + n] * wr[b, pl.ds(s, 1), :]
                    inner = term if inner is None else inner + term
            if inner is not None:
                moved = inner if c == 0 else pltpu.roll(inner, BLOCK - c, 1)
                total = moved if total is None else total + moved
        return (wr[b, pl.ds(A * GROUP, 1), :] + eig_t[eig, :]) * field - total

    zero = jnp.zeros((K, BLOCK), jnp.float32)
    sums = (zero, zero)
    for t in range(T):
        q = order(t, core)

        def first_pass(i, carry):
            b = q * CB + i
            field = ext1[HALO + b]
            value = operate(ext1, b, field)
            ext2[HALO + b] = value
            image[chip, b] = value
            return (carry[0] + field * field, carry[1] + value * value)

        sums = lax.fori_loop(0, CB, first_pass, sums)
        for j in range(1, X):
            to = lax.rem(chip + j, X)
            remote(
                image.at[chip, pl.ds(q * CB, CB)], image.at[chip, pl.ds(q * CB, CB)],
                im_send.at[t, j - 1], im_recv.at[q, chip], lat, to * CORES + core,
            )
        halo_send(ext2, q, h2_send, h2_recv)

    ones = jnp.ones((8, BLOCK), jnp.float32)

    def lanes(values):
        return lax.dot_general(
            ones, values, (((1,), (1,)), ((), ())), precision=HIGHEST,
            preferred_element_type=jnp.float32,
        )

    def lat_send(buf, send, recv):
        for j in range(1, L):
            remote(
                buf.at[lat], buf.at[lat], send.at[j - 1], recv.at[lat], lax.rem(lat + j, L), rad
            )

    def lat_sum(buf, send, recv):
        for j in range(1, L):
            l = lax.rem(lat + j, L)
            arrived(buf.at[l], send.at[j - 1], recv.at[l])
        total = buf[0]
        for l in range(1, L):
            total = total + buf[l]
        return total

    def put(buf, at, value):
        width = value.shape[1]
        if width < BLOCK:
            value = jnp.concatenate(
                [value, jnp.zeros((8, BLOCK - width), jnp.float32)], axis=1
            )
        buf[at] = value

    put(s1, lat, lanes(jnp.concatenate(sums, axis=0)))
    lat_send(s1, s1_send, s1_recv)

    for j in range(1, X):
        other = lax.rem(chip + j, X)
        other_rows = to_ref[pl.ds(pl.multiple_of(other * K, 8), K), :]
        for q in range(T):
            product = dot(other_rows, gathered[q])
            for i in range(CB):
                modal[other, q * CB + i] = product[:, i * BLOCK:(i + 1) * BLOCK]

    s2[rad] = lat_sum(s1, s1_send, s1_recv)
    for j in range(1, R):
        remote(
            s2.at[rad], s2.at[rad], s2_send.at[j - 1], s2_recv.at[rad], lat, lax.rem(rad + j, R)
        )
    for j in range(1, R):
        r = lax.rem(rad + j, R)
        arrived(s2.at[r], s2_send.at[j - 1], s2_recv.at[r])
    for x in range(X):
        line = s2[CORES * x]
        for c in range(1, CORES):
            line = line + s2[CORES * x + c]
        column = jnp.transpose(jnp.broadcast_to(line[0:1, :], (BLOCK, BLOCK)))
        base, power = column[0:K], column[K:2 * K]
        upper = 1.5 * jnp.sqrt(power / (base + 1e-06))
        lower = upper * 0.125
        center = (upper + lower) * 0.5
        half_width = (upper - lower) * 0.5
        sigma = center / half_width
        rho_zero = 1.0 / sigma
        rho_one = 1.0 / (2.0 * sigma - rho_zero)
        second = 2.0 * rho_one / half_width
        coef[x, 0] = (1.0 + rho_one * rho_zero) / center + second
        coef[x, 1] = -second / center

    mine = jnp.concatenate(
        [
            from_ref[pl.ds(pl.multiple_of(rad * slab, 8), slab), :],
            from_ref[pl.ds(pl.multiple_of(partner * slab, 8), slab), :],
        ],
        axis=0,
    )

    def columns(q):
        return out.at[:, pl.ds(pl.multiple_of(core * half + q * CW, BLOCK), CW)]

    def their_columns(q):
        return out.at[:, pl.ds(pl.multiple_of((1 - core) * half + q * CW, BLOCK), CW)]

    def finish(t):
        q = order(t, core)
        for j in range(1, X):
            x = lax.rem(chip + j, X)
            arrived(image.at[x, pl.ds(q * CB, CB)], im_send.at[t, j - 1], im_recv.at[q, x])
        blocks = []
        for i in range(CB):
            b = q * CB + i
            blocks.append(
                jnp.concatenate(
                    [coef[x, 0] * modal[x, b] + coef[x, 1] * image[x, b] for x in range(X)], axis=0
                )
            )
        product = dot(mine, jnp.concatenate(blocks, axis=1))
        part[q, 0] = product[0:slab]
        part[q, 1] = product[slab:K]
        remote(part.at[q, 1], columns(q), out_send.at[q], out_recv.at[q], lat, partner)
        pltpu.make_async_copy(part.at[q, 0], columns(q), out_sem.at[q]).start()

    finish(0)

    halo_wait(ext2, h2_send, h2_recv)
    spread_halo(ext2)

    def spread_own(b, carry):
        spread(ext2, HALO + b, ext2[HALO + b])
        return carry

    lax.fori_loop(0, NB, spread_own, 0)

    def second_pass(b, carry):
        field = ext2[HALO + b]
        value = operate(ext2, b, field)
        final = modal[chip, b] - (coef[chip, 0] * field + coef[chip, 1] * value)
        return carry + final * final

    squares = lax.fori_loop(0, NB, second_pass, zero)
    put(s3, lat, lanes(squares))
    lat_send(s3, s3_send, s3_recv)

    for t in range(1, T):
        finish(t)

    s4[core] = lat_sum(s3, s3_send, s3_recv)
    remote(s4.at[core], s4.at[core], s4_send, s4_recv, lat, partner)
    arrived(s4.at[1 - core], s4_send, s4_recv)
    base_line = s2[CORES * chip] + s2[CORES * chip + 1]
    norm = jnp.sqrt((s4[0] + s4[1]) / (base_line + 1e-06))
    res_ref[...] = jnp.where(core == 0, norm[0:1, 0:slab], norm[0:1, slab:2 * slab])

    for q in range(T):
        pltpu.make_async_copy(part.at[q, 0], columns(q), out_sem.at[q]).wait()
        arrived(their_columns(q), out_send.at[q], out_recv.at[q])
    for copy in pending:
        copy.wait_send()


def on_device(L, R, source, to_modes, from_modes, eigenvalue, shifts, weights, neighbors):
    slab, nodes = source.shape
    S = weights.shape[0]
    levels = to_modes.shape[0]
    T, X, K = CHUNKS, R // CORES, slab * CORES
    half = nodes // CORES
    NB = half // BLOCK
    CW = half // T
    E = NB + 2 * HALO
    A = -(-S // GROUP)
    f32 = jnp.float32
    dma = pltpu.SemaphoreType.DMA
    vmem = pl.BlockSpec(memory_space=pltpu.VMEM)
    anywhere = pl.BlockSpec(memory_space=pl.ANY)
    smoothed, norm = pl.pallas_call(
        functools.partial(kernel, L, R, S),
        name="smoother",
        out_shape=(
            jax.ShapeDtypeStruct((slab, nodes), f32),
            jax.ShapeDtypeStruct((1, slab), f32),
        ),
        in_specs=[
            anywhere, anywhere, vmem, vmem, vmem, vmem, pl.BlockSpec(memory_space=pltpu.SMEM),
        ],
        out_specs=(anywhere, vmem),
        scratch_shapes=[
            pltpu.VMEM((T, levels, CW), f32),
            pltpu.VMEM((S, half), f32),
            pltpu.VMEM((NB, (A + 1) * GROUP, BLOCK), f32),
            pltpu.VMEM((A * E, K, BLOCK), f32),
            pltpu.VMEM((A * E, K, BLOCK), f32),
            pltpu.VMEM((X, NB, K, BLOCK), f32),
            pltpu.VMEM((X, NB, K, BLOCK), f32),
            pltpu.VMEM((levels, levels), f32),
            pltpu.VMEM((X, 2, K, BLOCK), f32),
            pltpu.VMEM((T, 2, slab, CW), f32),
            pltpu.VMEM((NB, BLOCK), f32),
            pltpu.VMEM((L, 8, BLOCK), f32),
            pltpu.VMEM((R, 8, BLOCK), f32),
            pltpu.VMEM((L, 8, BLOCK), f32),
            pltpu.VMEM((CORES, 8, BLOCK), f32),
            dma((T,)), dma(()),
            dma((T, R - 1)), dma((T, R)),
            dma((T,)), dma((T,)), dma((T,)), dma((T,)),
            dma((T, max(X - 1, 1))), dma((T, X)),
            dma((L - 1,)), dma((L,)), dma((R - 1,)), dma((R,)),
            dma((L - 1,)), dma((L,)), dma(()), dma(()),
            dma((T,)), dma((T,)), dma((T,)),
        ],
        compiler_params=pltpu.CompilerParams(
            collective_id=0, has_side_effects=True, vmem_limit_bytes=48 * 1024 * 1024
        ),
    )(
        source, weights, to_modes, from_modes, eigenvalue.reshape(1, levels),
        shifts.reshape(nodes // BLOCK, BLOCK), neighbors,
    )
    return smoothed, norm.reshape(slab)


def solution(mesh):
    return jax.shard_map(
        functools.partial(on_device, mesh.shape["lat"], mesh.shape["rad"]),
        mesh=mesh,
        in_specs=(P("rad", "lat"), P(), P(), P(), P("lat"), P(None, "lat"), P(None, "lat")),
        out_specs=(P("rad", "lat"), P("rad")),
        check_vma=False,
    )
```

time: 225 us -> 54.4 us (0.24); the launches traced: 222 us -> 53.9 us
  other arithmetic: 53 us -> 0 us
  Pallas kernels: 0 us -> 46.1 us
  blocking collectives: 42.5 us -> 0 us
  local copies, waits for them, and re-layouts: 48.7 us -> 7.15 us
  waiting for transfers between devices: 31.6 us -> 0 us
  matrix products: 20.7 us -> 0 us
  between operations: 15.1 us -> 0.66 us
  starting transfers between devices: 9.93 us -> 0 us
    pallas_call x0 -> x1, Pallas kernels: none -> 46.1 us  [on_device(): pl.pallas_call(functools.partial(kernel, L, R, S), name='smoother', out_s...]
    psum x2 -> x0, blocking collectives: 42.5 us -> none  [the longest x1 22 us: on_device(): squares = lax.psum(jnp.sum(final_res * final_res, axis=1), 'lat')]
    reduce_sum x4 -> x0, other arithmetic: 29.2 us -> none  [the longest x1 13.6 us: on_device(): jnp.sum(image * image, axis=1)]
    reduce_scatter x1 -> x0, waiting for transfers between devices: 25.6 us -> none  [on_device(): lax.psum_scatter(jnp.dot(level_cols, source, precision=lax.Precision.HIGH...]
    slice x66 -> x0, local copies, waits for them, and re-layouts: 22.6 us -> none  [the longest x62 16.5 us: operate(): moved = jnp.roll(picked[slot_index], -(slot_index % BLOCK), axis=2)]
    dot_general x4 -> x0, matrix products: 20.7 us -> none  [the longest x2 13.1 us: operate(): jnp.einsum('sjc,kcb->skjb', selector, ext_blocks, precision=lax.Precision...]
    concatenate x60 -> x0, other arithmetic: 13.7 us -> none  [operate(): moved = jnp.roll(picked[slot_index], -(slot_index % BLOCK), axis=2)]
    squeeze x2 -> x0, local copies, waits for them, and re-layouts: 11.1 us -> none  [operate(): moved = jnp.roll(picked[slot_index], -(slot_index % BLOCK), axis=2)]
  transfers between devices with their start and end apart: 6 -> 0, of which waited for: 4 -> 0; matrix products, arithmetic and copies ran while one was open for 25% -> 0% of each run, Pallas kernels for 0% -> 0%
where the time goes in v1:
time: 54.4 us; the launch traced here: 53.9 us
  Pallas kernels  46.1 us (85%)
  local copies, waits for them, and re-layouts  7.15 us (13%)
  between operations  0.66 us (1%)
    pallas_call x1, Pallas kernels, on_device(): pl.pallas_call(functools.partial(kernel, L, R, S), name='smoother', out_s...  46.1 us
    unnamed x16, local copies, waits for them, and re-layouts  7.15 us

profile of v1, /device:TPU:0, one launch (start us, length us, event | category | flops | bytes accessed | tf_op | source)
XLA Modules:
  0.0 53.9 jit_solution(6435404114313061809)
XLA Ops:
  0.6 0.0 copy-start.6
  0.6 0.6 %copy-done.6 = f32[128]{0:T(128)S(1)} copy-done((f32[128]{0:T(128)S(1)}, f32[128]{0:T(128)}, u32[]{:S(2)}) %copy-start.6) | copy-done | bytes 536
  1.3 0.0 copy-start
  1.3 1.0 %copy-done = f32[32,4096]{1,0:T(8,128)S(1)} copy-done((f32[32,4096]{1,0:T(8,128)S(1)}, f32[32,4096]{1,0:T(8,128)}, u32[]{:S(2)}) %copy-start) | copy-done | bytes 524312
  2.3 0.0 copy-start.1
  2.3 1.0 %copy-done.1 = f32[31,4096]{1,0:T(8,128)S(1)} copy-done((f32[31,4096]{1,0:T(8,128)S(1)}, f32[31,4096]{1,0:T(8,128)}, u32[]{:S(2)}) %copy-start.1) | copy-done | bytes 507928
  3.4 0.0 copy-start.2
  3.4 0.8 %copy-done.2 = f32[128,128]{1,0:T(8,128)S(1)} copy-done((f32[128,128]{1,0:T(8,128)S(1)}, f32[128,128]{1,0:T(8,128)}, u32[]{:S(2)}) %copy-start.2) | copy-done | bytes 65560
  4.2 0.0 copy-start.3
  4.2 0.8 %copy-done.3 = f32[128,128]{1,0:T(8,128)S(1)} copy-done((f32[128,128]{1,0:T(8,128)S(1)}, f32[128,128]{1,0:T(8,128)}, u32[]{:S(2)}) %copy-start.3) | copy-done | bytes 65560
  5.1 0.0 copy-start.4
  5.1 0.7 %copy-done.4 = f32[4096]{0:T(1024)S(1)} copy-done((f32[4096]{0:T(1024)S(1)}, f32[4096]{0:T(1024)}, u32[]{:S(2)}) %copy-start.4) | copy-done | bytes 16408
  5.8 0.0 copy-start.5
  5.8 0.7 %copy-done.5 = s32[31,32]{1,0:T(8,128)S(1)} copy-done((s32[31,32]{1,0:T(8,128)S(1)}, s32[31,32]{1,0:T(8,128)}, u32[]{:S(2)}) %copy-start.5) | copy-done | bytes 3992
  6.5 46.1 %smoother.1 = (f32[32,4096]{1,0:T(8,128)S(1)}, f32[1,32]{1,0:T(1,128)S(1)}) custom-call(f32[32,4096]{1,0:T(8,128)S(1)} %copy-done, f32[31,4096]{1,0:T(8,128)S(1)} %copy-done.1, f32[128,128]{1,0:T(8,128)S(1)} %copy-done.2, f32[128,128]{1,0:T(8,128)S(1)} %copy-done.3, f32[1,128]{1,0:T(1,128)S(1)} %bitcast.4, f32[32,128]{1,0:T(8,128)S(1)} %bitcast.3, ...), custom_call_target="tpu_custom_call" | custom-call | tf_op jit(solution)/shard_map/smoother/pallas_call | solution.py:366
  52.6 0.8 %copy.11 = f32[32,4096]{1,0:T(8,128)} copy(f32[32,4096]{1,0:T(8,128)S(1)} %get-tuple-element.8) | data formatting | bytes 1048576
  53.4 0.5 copy.12
Async XLA Ops:
  0.6 0.7 %copy-start.6 = (f32[128]{0:T(128)S(1)}, f32[128]{0:T(128)}, u32[]{:S(2)}) copy-start(f32[128]{0:T(128)} %param.10) | copy-start | bytes 1540
  1.3 1.0 %copy-start = (f32[32,4096]{1,0:T(8,128)S(1)}, f32[32,4096]{1,0:T(8,128)}, u32[]{:S(2)}) copy-start(f32[32,4096]{1,0:T(8,128)} %src.1) | copy-start | bytes 1572868
  2.3 1.0 %copy-start.1 = (f32[31,4096]{1,0:T(8,128)S(1)}, f32[31,4096]{1,0:T(8,128)}, u32[]{:S(2)}) copy-start(f32[31,4096]{1,0:T(8,128)} %w_hbm.1) | copy-start | bytes 1523716
  3.4 0.8 %copy-start.2 = (f32[128,128]{1,0:T(8,128)S(1)}, f32[128,128]{1,0:T(8,128)}, u32[]{:S(2)}) copy-start(f32[128,128]{1,0:T(8,128)} %to_ref.1) | copy-start | bytes 196612
  4.2 0.8 %copy-start.3 = (f32[128,128]{1,0:T(8,128)S(1)}, f32[128,128]{1,0:T(8,128)}, u32[]{:S(2)}) copy-start(f32[128,128]{1,0:T(8,128)} %from_ref.1) | copy-start | bytes 196612
  5.1 0.7 %copy-start.4 = (f32[4096]{0:T(1024)S(1)}, f32[4096]{0:T(1024)}, u32[]{:S(2)}) copy-start(f32[4096]{0:T(1024)} %param.11) | copy-start | bytes 49156
  5.8 0.7 %copy-start.5 = (s32[31,32]{1,0:T(8,128)S(1)}, s32[31,32]{1,0:T(8,128)}, u32[]{:S(2)}) copy-start(s32[31,32]{1,0:T(8,128)} %nbr_ref.1) | copy-start | bytes 11908

commit v2 on v1

--- a/solution.py
+++ b/solution.py
@@ -22,10 +22,10 @@
 
 def kernel(
     L, R, S,
-    src, w_hbm, to_ref, from_ref, eig_ref, shift_ref, nbr_ref,
+    src, w_hbm, to_hbm, from_hbm, eig_hbm, shift_hbm, nbr_hbm,
     out, res_ref,
     gathered, wv, wr, ext1, ext2, modal, image, eig_t, coef, part, rows, s1, s2, s3, s4,
-    own_sem, w_sem, ag_send, ag_recv, h1_send, h1_recv, h2_send, h2_recv, im_send, im_recv,
+    to_ref, from_ref, eig_ref, nbr_ref, in_sem, own_sem, w_sem, ag_send, ag_recv, h1_send, h1_recv, h2_send, h2_recv, im_send, im_recv,
     s1_send, s1_recv, s2_send, s2_recv, s3_send, s3_recv, s4_send, s4_recv,
     out_send, out_recv, out_sem,
 ):
@@ -60,9 +60,18 @@
     w_copy = pltpu.make_async_copy(
         w_hbm.at[:, pl.ds(pl.multiple_of(core * half, BLOCK), half)], wv, w_sem
     )
+    inputs = [
+        pltpu.make_async_copy(a, b, in_sem.at[i])
+        for i, (a, b) in enumerate([
+            (to_hbm, to_ref), (from_hbm, from_ref), (eig_hbm, eig_ref), (nbr_hbm, nbr_ref),
+            (shift_hbm.at[pl.ds(pl.multiple_of(core * NB, 8), NB), :], rows),
+        ])
+    ]
+    w_copy.start()
+    for copy in inputs:
+        copy.start()
     for q in range(T):
         own_copy(q).start()
-    w_copy.start()
 
     barrier = pltpu.get_barrier_semaphore()
     for j in range(1, R):
@@ -109,9 +118,9 @@
             )
 
     w_copy.wait()
+    for copy in inputs:
+        copy.wait()
     row_id = lax.broadcasted_iota(jnp.int32, (A * GROUP, BLOCK), 0)
-    shift_rows = shift_ref[pl.ds(pl.multiple_of(core * NB, 8), NB), :]
-    rows[...] = shift_rows
 
     def prepare(b, carry):
         wr[b, pl.ds((A - 1) * GROUP, GROUP), :] = jnp.zeros((GROUP, BLOCK), jnp.float32)
@@ -362,7 +371,7 @@
     f32 = jnp.float32
     dma = pltpu.SemaphoreType.DMA
     vmem = pl.BlockSpec(memory_space=pltpu.VMEM)
-    anywhere = pl.BlockSpec(memory_space=pl.ANY)
+    hbm = pl.BlockSpec(memory_space=pltpu.HBM)
     smoothed, norm = pl.pallas_call(
         functools.partial(kernel, L, R, S),
         name="smoother",
@@ -370,10 +379,8 @@
             jax.ShapeDtypeStruct((slab, nodes), f32),
             jax.ShapeDtypeStruct((1, slab), f32),
         ),
-        in_specs=[
-            anywhere, anywhere, vmem, vmem, vmem, vmem, pl.BlockSpec(memory_space=pltpu.SMEM),
-        ],
-        out_specs=(anywhere, vmem),
+        in_specs=[hbm] * 7,
+        out_specs=(hbm, vmem),
         scratch_shapes=[
             pltpu.VMEM((T, levels, CW), f32),
             pltpu.VMEM((S, half), f32),
@@ -390,7 +397,11 @@
             pltpu.VMEM((R, 8, BLOCK), f32),
             pltpu.VMEM((L, 8, BLOCK), f32),
             pltpu.VMEM((CORES, 8, BLOCK), f32),
-            dma((T,)), dma(()),
+            pltpu.VMEM((levels, levels), f32),
+            pltpu.VMEM((levels, levels), f32),
+            pltpu.VMEM((1, levels), f32),
+            pltpu.SMEM(neighbors.shape, jnp.int32),
+            dma((5,)), dma((T,)), dma(()),
             dma((T, R - 1)), dma((T, R)),
             dma((T,)), dma((T,)), dma((T,)), dma((T,)),
             dma((T, max(X - 1, 1))), dma((T, X)),
@@ -399,7 +410,7 @@
             dma((T,)), dma((T,)), dma((T,)),
         ],
         compiler_params=pltpu.CompilerParams(
-            collective_id=0, has_side_effects=True, vmem_limit_bytes=48 * 1024 * 1024
+            collective_id=0, has_side_effects=True, vmem_limit_bytes=67043328
         ),
     )(
         source, weights, to_modes, from_modes, eigenvalue.reshape(1, levels),

time: 54.4 us -> 49.3 us (0.906)
  local copies, waits for them, and re-layouts: 7.15 us -> 2.39 us
    unnamed x16 -> x4, local copies, waits for them, and re-layouts: 7.15 us -> 2.39 us
where the time goes in v2:
time: 49.3 us; the launch traced here: 49.1 us
  Pallas kernels  46.1 us (94%)
  local copies, waits for them, and re-layouts  2.39 us (5%)
  between operations  0.65 us (1%)
    pallas_call x1, Pallas kernels, on_device(): pl.pallas_call(functools.partial(kernel, L, R, S), name='smoother', out_s...  46.1 us
    unnamed x4, local copies, waits for them, and re-layouts  2.39 us

profile of v2, /device:TPU:0, one launch (start us, length us, event | category | flops | bytes accessed | tf_op | source)
XLA Modules:
  0.0 49.1 jit_solution(3715668572287311749)
XLA Ops:
  0.6 46.1 %smoother.1 = (f32[32,4096]{1,0:T(8,128)}, f32[1,32]{1,0:T(1,128)}) custom-call(f32[32,4096]{1,0:T(8,128)} %src.1, f32[31,4096]{1,0:T(8,128)} %w_hbm.1, f32[128,128]{1,0:T(8,128)} %to_hbm.1, f32[128,128]{1,0:T(8,128)} %from_hbm.1, f32[1,128]{1,0:T(1,128)} %bitcast.4, f32[32,128]{1,0:T(8,128)} %bitcast.3, s32[31,32]{1,0:T(8,128)} %nbr_hbm.1), custom_call_target="tpu_custom_call" | custom-call | tf_op jit(solution)/shard_map/smoother/pallas_call | solution.py:375
  46.7 0.0 copy-start
  46.7 1.9 %copy.11 = f32[32,4096]{1,0:T(8,128)} copy(f32[32,4096]{1,0:T(8,128)} %get-tuple-element.8) | data formatting | bytes 1048576
  48.6 0.0 copy-done
  48.6 0.5 %copy.12 = f32[32]{0:T(128)} copy(f32[32]{0:T(128)S(1)} %bitcast.5) | data formatting | bytes 256
Async XLA Ops:
  46.7 1.9 %copy-start = (f32[1,32]{1,0:T(1,128)S(1)}, f32[1,32]{1,0:T(1,128)}, u32[]{:S(2)}) copy-start(f32[1,32]{1,0:T(1,128)} %get-tuple-element.5) | copy-start | bytes 388

commit v3 on v2

v3 whole, which is shorter than its diff:
```python
import functools

import jax
import jax.numpy as jnp
from jax import lax
from jax.experimental import pallas as pl
from jax.experimental.pallas import tpu as pltpu
from jax.sharding import PartitionSpec as P

BLOCK = 128
HALO = 8
CHUNKS = 4
GROUP = 8
CORES = 2
HIGHEST = lax.Precision.HIGHEST
MESH = pl.DeviceIdType.MESH


def dot(a, b):
    return jnp.dot(a, b, precision=HIGHEST, preferred_element_type=jnp.float32)


def kernel(
    L, R, S,
    src, w_hbm, to_hbm, from_hbm, eig_hbm, shift_hbm, nbr_hbm,
    out, res_ref,
    gathered, wv, wr, outer1, inner1, outer2, inner2, others, modal, image, eig_t, coef, part,
    rows, s1, s2, s3, to_ref, from_ref, eig_ref, nbr_ref,
    in_sem, own_sem, w_sem, ag_send, ag_recv,
    o1_send, o1_recv, i1_send, i1_recv, o2_send, o2_recv, i2_send, i2_recv, x_send, x_recv,
    im_send, im_recv, s1_send, s1_recv, s2_send, s2_recv, s3_send, s3_recv,
    out_send, out_recv, out_sem,
):
    T = CHUNKS
    X = R // CORES
    M = L * CORES
    slab, nodes = src.shape
    K = slab * CORES
    half = nodes // CORES
    NB = half // BLOCK
    CB = NB // T
    HC = HALO // CB
    CW = CB * BLOCK
    E = NB + HALO
    A = -(-S // GROUP)
    lat = lax.axis_index("lat")
    rad = lax.axis_index("rad")
    core = lax.rem(rad, CORES)
    chip = lax.div(rad, CORES)
    partner = chip * CORES + (1 - core)
    me = lat * CORES + core
    other_lat = lax.rem(lat + (L - 1) * (1 - core) + core, L)

    def order(t, c):
        return t * (1 - c) + (T - 1 - t) * c

    def own_copy(q):
        return pltpu.make_async_copy(
            src.at[:, pl.ds(pl.multiple_of(core * half + q * CW, BLOCK), CW)],
            gathered.at[q, pl.ds(pl.multiple_of(rad * slab, 8), slab), :],
            own_sem.at[q],
        )

    w_copy = pltpu.make_async_copy(
        w_hbm.at[:, pl.ds(pl.multiple_of(core * half, BLOCK), half)], wv, w_sem
    )
    inputs = [
        pltpu.make_async_copy(a, b, in_sem.at[i])
        for i, (a, b) in enumerate([
            (to_hbm, to_ref), (from_hbm, from_ref), (eig_hbm, eig_ref), (nbr_hbm, nbr_ref),
            (shift_hbm.at[pl.ds(pl.multiple_of(core * NB, 8), NB), :], rows),
        ])
    ]

    def plane_peer(j):
        m = lax.rem(me + j, M)
        return m, lax.div(m, CORES), chip * CORES + lax.rem(m, CORES)

    barrier = pltpu.get_barrier_semaphore()
    for j in range(1, R):
        r = lax.rem(rad + j, R)
        pl.semaphore_signal(
            barrier, inc=1, device_id={"lat": lat, "rad": r}, device_id_type=MESH
        )
    for j in range(1, M):
        m, to_lat, to_rad = plane_peer(j)
        pl.semaphore_signal(
            barrier, inc=1, device_id={"lat": to_lat, "rad": to_rad}, device_id_type=MESH
        )
    w_copy.start()
    for copy in inputs:
        copy.start()
    for q in range(T):
        own_copy(q).start()
    pl.semaphore_wait(barrier, R - 1 + M - 1)

    pending = []

    def remote(src_ref, dst_ref, send, recv, lat_to, rad_to):
        copy = pltpu.make_async_remote_copy(
            src_ref=src_ref, dst_ref=dst_ref, send_sem=send, recv_sem=recv,
            device_id={"lat": lat_to, "rad": rad_to}, device_id_type=MESH,
        )
        copy.start()
        pending.append(copy)

    def arrived(dst_ref, send, recv):
        pltpu.make_async_remote_copy(
            src_ref=dst_ref, dst_ref=dst_ref, send_sem=send, recv_sem=recv,
            device_id={"lat": lat, "rad": partner}, device_id_type=MESH,
        ).wait_recv()

    def slot(q, r):
        return gathered.at[q, pl.ds(pl.multiple_of(r * slab, 8), slab), :]

    for t in range(T):
        for j in range(1, R):
            to = lax.rem(rad + j, R)
            to_core = lax.rem(to, CORES)
            q = order(t, to_core)
            remote(
                src.at[:, pl.ds(pl.multiple_of(to_core * half + q * CW, BLOCK), CW)],
                slot(q, rad), ag_send.at[t, j - 1], ag_recv.at[q, rad], lat, to,
            )

    w_copy.wait()
    for copy in inputs:
        copy.wait()
    row_id = lax.broadcasted_iota(jnp.int32, (A * GROUP, BLOCK), 0)

    def prepare(b, carry):
        wr[b, pl.ds((A - 1) * GROUP, GROUP), :] = jnp.zeros((GROUP, BLOCK), jnp.float32)
        wr[b, pl.ds(0, S), :] = wv[:, pl.ds(pl.multiple_of(b * BLOCK, BLOCK), BLOCK)]
        tile = wr[b, pl.ds(0, A * GROUP), :]
        placed = tile
        for c in range(1, GROUP):
            placed = jnp.where(lax.rem(row_id, GROUP) == c, pltpu.roll(tile, c, 1), placed)
        wr[b, pl.ds(0, A * GROUP), :] = placed
        diagonal = jnp.sum(tile, axis=0, keepdims=True) + rows[pl.ds(b, 1), :]
        wr[b, pl.ds(A * GROUP, GROUP), :] = jnp.broadcast_to(diagonal, (GROUP, BLOCK))
        return carry

    lax.fori_loop(0, NB, prepare, 0)
    levels = to_ref.shape[0]
    eig_t[...] = jnp.transpose(jnp.broadcast_to(eig_ref[...], (levels, levels)))

    o_at = HALO * (1 - core)
    i_at = HALO * core

    def outer_dst(c, q):
        return (1 - c) * (NB + q * CB) + c * (q * CB - NB + HALO)

    def inner_dst(c, q):
        return c * (NB + q * CB) + (1 - c) * (q * CB - NB + HALO)

    def outer_send(buf, t, send, recv):
        q = order(t, core)
        remote(
            buf.at[pl.ds(o_at + q * CB, CB)], buf.at[pl.ds(outer_dst(core, q), CB)],
            send.at[t], recv.at[t], other_lat, partner,
        )

    def outer_wait(buf, send, recv):
        for t in range(HC):
            at = outer_dst(1 - core, order(t, 1 - core))
            arrived(buf.at[pl.ds(at, CB)], send.at[t], recv.at[t])

    def inner_send(buf, base, t, send, recv):
        q = order(t, core)
        remote(
            buf.at[pl.ds(base + i_at + q * CB, CB)],
            buf.at[pl.ds(base + inner_dst(core, q), CB)],
            send.at[t - (T - HC)], recv.at[t - (T - HC)], lat, partner,
        )

    def inner_wait(buf, base, send, recv):
        for t in range(T - HC, T):
            at = inner_dst(1 - core, order(t, 1 - core))
            arrived(buf.at[pl.ds(base + at, CB)], send.at[t - (T - HC)], recv.at[t - (T - HC)])

    def spread_at(targets, value):
        for a in range(1, A):
            moved = pltpu.roll(value, BLOCK - a * GROUP, 1)
            for buf, k in targets:
                buf[a * E + k] = moved

    def spread_halo(buf, base, at):
        def step(k, carry):
            spread_at([(buf, base + at + k)], buf[base + at + k])
            return carry

        lax.fori_loop(0, HALO, step, 0)

    outer_halo = core * NB
    inner_halo = (1 - core) * NB

    def own_rows(x):
        return to_ref[pl.ds(pl.multiple_of(x * K, 8), K), :]

    def project_others(t):
        q = order(t, core)
        for j in range(1, X):
            x = lax.rem(chip + j, X)
            base = (j - 1) * A * E
            product = dot(own_rows(x), gathered[q])
            for i in range(CB):
                value = product[:, i * BLOCK:(i + 1) * BLOCK]
                modal[x, q * CB + i] = value
                others[base + i_at + q * CB + i] = value
            if t >= T - HC:
                inner_send(others, base, t, x_send.at[j - 1], x_recv.at[j - 1])
            for i in range(CB):
                spread_at(
                    [(others, base + i_at + q * CB + i)], product[:, i * BLOCK:(i + 1) * BLOCK]
                )

    for t in range(T):
        q = order(t, core)
        own_copy(q).wait()
        for j in range(1, R):
            r = lax.rem(rad + j, R)
            arrived(slot(q, r), ag_send.at[t, j - 1], ag_recv.at[q, r])
        product = dot(own_rows(chip), gathered[q])
        for i in range(CB):
            value = product[:, i * BLOCK:(i + 1) * BLOCK]
            b = q * CB + i
            outer1[o_at + b] = value
            inner1[i_at + b] = value
            modal[chip, b] = value
        if t < HC:
            outer_send(outer1, t, o1_send, o1_recv)
        if t >= T - HC:
            inner_send(inner1, 0, t, i1_send, i1_recv)
        for i in range(CB):
            b = q * CB + i
            spread_at(
                [(outer1, o_at + b), (inner1, i_at + b)], product[:, i * BLOCK:(i + 1) * BLOCK]
            )
        if t < T - 1:
            project_others(t)
        if t == T - 2:
            outer_wait(outer1, o1_send, o1_recv)
            spread_halo(outer1, 0, outer_halo)

    def operate(buf, base, x, b, field):
        total = None
        for c in range(GROUP):
            inner = None
            for a in range(A):
                s = a * GROUP + c
                if s < S:
                    n = nbr_ref[s, core * NB + b]
                    term = buf[base + a * E + b + n] * wr[b, pl.ds(s, 1), :]
                    inner = term if inner is None else inner + term
            if inner is not None:
                moved = inner if c == 0 else pltpu.roll(inner, BLOCK - c, 1)
                total = moved if total is None else total + moved
        eig = eig_t[pl.ds(pl.multiple_of(x * K, 8), K), :]
        return (wr[b, pl.ds(A * GROUP, 1), :] + eig) * field - total

    def first_pass(buf, at):
        def step(b, carry):
            field = modal[chip, b]
            value = operate(buf, at, chip, b, field)
            outer2[o_at + b] = value
            inner2[i_at + b] = value
            image[chip, b] = value
            return (carry[0] + field * field, carry[1] + value * value)

        return step

    zero = jnp.zeros((K, BLOCK), jnp.float32)
    sums = (zero, zero)
    for t in range(T):
        q = order(t, core)
        if t == T // 2:
            inner_wait(inner1, 0, i1_send, i1_recv)
            spread_halo(inner1, 0, inner_halo)
        step = first_pass(outer1, o_at) if t < T // 2 else first_pass(inner1, i_at)
        sums = lax.fori_loop(q * CB, (q + 1) * CB, step, sums)
        if t < HC:
            outer_send(outer2, t, o2_send, o2_recv)
        if t < T // 2:
            for j in range(1, X):
                to = lax.rem(chip + j, X)
                remote(
                    image.at[chip, pl.ds(q * CB, CB)], image.at[chip, pl.ds(q * CB, CB)],
                    im_send.at[t, j - 1], im_recv.at[q, chip], lat, to * CORES + core,
                )
        if t >= T - HC:
            inner_send(inner2, 0, t, i2_send, i2_recv)

    ones = jnp.ones((8, BLOCK), jnp.float32)

    def lanes(values):
        line = lax.dot_general(
            ones, values, (((1,), (1,)), ((), ())), precision=HIGHEST,
            preferred_element_type=jnp.float32,
        )
        width = line.shape[1]
        if width < BLOCK:
            line = jnp.concatenate(
                [line, jnp.zeros((8, BLOCK - width), jnp.float32)], axis=1
            )
        return line[0:1]

    def plane_send(buf, send, recv):
        for j in range(1, M):
            m, to_lat, to_rad = plane_peer(j)
            remote(buf.at[me], buf.at[me], send.at[j - 1], recv.at[me], to_lat, to_rad)

    def plane_sum(buf, send, recv):
        for j in range(1, M):
            m = lax.rem(me + j, M)
            arrived(buf.at[m], send.at[j - 1], recv.at[m])
        total = buf[0]
        for m in range(1, M):
            total = total + buf[m]
        return total

    s1[me] = lanes(jnp.concatenate(sums, axis=0))
    plane_send(s1, s1_send, s1_recv)
    project_others(T - 1)

    s2[chip] = plane_sum(s1, s1_send, s1_recv)
    for j in range(1, X):
        x = lax.rem(chip + j, X)
        remote(
            s2.at[chip], s2.at[chip], s2_send.at[j - 1], s2_recv.at[chip], lat, x * CORES + core
        )

    inside = (NB // 2) * (1 - core)
    for j in range(1, X):
        x = lax.rem(chip + j, X)
        base = (j - 1) * A * E
        inner_wait(others, base, x_send.at[j - 1], x_recv.at[j - 1])
        spread_halo(others, base, inner_halo)
    for j in range(1, X):
        x = lax.rem(chip + j, X)
        base = (j - 1) * A * E

        def others_pass(b, carry, x=x, base=base):
            image[x, b] = operate(others, base + i_at, x, b, modal[x, b])
            return carry

        lax.fori_loop(inside, inside + NB // 2, others_pass, 0)

    for j in range(1, X):
        x = lax.rem(chip + j, X)
        arrived(s2.at[x], s2_send.at[j - 1], s2_recv.at[x])
    for x in range(X):
        column = jnp.transpose(jnp.broadcast_to(s2[x], (BLOCK, BLOCK)))
        base, power = column[0:K], column[K:2 * K]
        upper = 1.5 * jnp.sqrt(power / (base + 1e-06))
        lower = upper * 0.125
        center = (upper + lower) * 0.5
        half_width = (upper - lower) * 0.5
        sigma = center / half_width
        rho_zero = 1.0 / sigma
        rho_one = 1.0 / (2.0 * sigma - rho_zero)
        second = 2.0 * rho_one / half_width
        coef[x, 0] = (1.0 + rho_one * rho_zero) / center + second
        coef[x, 1] = -second / center

    mine = jnp.concatenate(
        [
            from_ref[pl.ds(pl.multiple_of(rad * slab, 8), slab), :],
            from_ref[pl.ds(pl.multiple_of(partner * slab, 8), slab), :],
        ],
        axis=0,
    )

    def columns(q):
        return out.at[:, pl.ds(pl.multiple_of(core * half + q * CW, BLOCK), CW)]

    def their_columns(q):
        return out.at[:, pl.ds(pl.multiple_of((1 - core) * half + q * CW, BLOCK), CW)]

    def finish(t):
        q = order(t, core)
        if t < T // 2:
            for j in range(1, X):
                x = lax.rem(chip + j, X)
                arrived(image.at[x, pl.ds(q * CB, CB)], im_send.at[t, j - 1], im_recv.at[q, x])
        blocks = []
        for i in range(CB):
            b = q * CB + i
            blocks.append(
                jnp.concatenate(
                    [coef[x, 0] * modal[x, b] + coef[x, 1] * image[x, b] for x in range(X)], axis=0
                )
            )
        product = dot(mine, jnp.concatenate(blocks, axis=1))
        part[q, 0] = product[0:slab]
        part[q, 1] = product[slab:K]
        remote(part.at[q, 1], columns(q), out_send.at[q], out_recv.at[q], lat, partner)
        pltpu.make_async_copy(part.at[q, 0], columns(q), out_sem.at[q]).start()

    def second_pass(buf, at):
        def step(b, carry):
            field = image[chip, b]
            value = operate(buf, at, chip, b, field)
            final = modal[chip, b] - (coef[chip, 0] * field + coef[chip, 1] * value)
            return carry + final * final

        return step

    def spread_own(b, carry):
        spread_at([(outer2, o_at + b), (inner2, i_at + b)], image[chip, b])
        return carry

    lax.fori_loop(0, NB, spread_own, 0)
    inner_wait(inner2, 0, i2_send, i2_recv)
    spread_halo(inner2, 0, inner_halo)
    squares = lax.fori_loop(inside, inside + NB // 2, second_pass(inner2, i_at), zero)
    for t in range(T // 2, T):
        finish(t)
    finish(0)

    outer_wait(outer2, o2_send, o2_recv)
    spread_halo(outer2, 0, outer_halo)
    outside = (NB // 2) * core
    squares = lax.fori_loop(outside, outside + NB // 2, second_pass(outer2, o_at), squares)
    s3[me] = lanes(squares)
    plane_send(s3, s3_send, s3_recv)
    for t in range(1, T // 2):
        finish(t)

    norm = jnp.sqrt(plane_sum(s3, s3_send, s3_recv) / (s2[chip] + 1e-06))
    res_ref[...] = jnp.where(core == 0, norm[:, 0:slab], norm[:, slab:2 * slab])

    for q in range(T):
        pltpu.make_async_copy(part.at[q, 0], columns(q), out_sem.at[q]).wait()
        arrived(their_columns(q), out_send.at[q], out_recv.at[q])
    for copy in pending:
        copy.wait_send()


def on_device(L, R, source, to_modes, from_modes, eigenvalue, shifts, weights, neighbors):
    slab, nodes = source.shape
    S = weights.shape[0]
    levels = to_modes.shape[0]
    T, X, K = CHUNKS, R // CORES, slab * CORES
    half = nodes // CORES
    NB = half // BLOCK
    CW = half // T
    E = NB + HALO
    A = -(-S // GROUP)
    M = L * CORES
    HC = HALO // (NB // T)
    f32 = jnp.float32

    def window(count):
        return pltpu.VMEM((count * A * E, K, BLOCK), f32)

    dma = pltpu.SemaphoreType.DMA
    vmem = pl.BlockSpec(memory_space=pltpu.VMEM)
    hbm = pl.BlockSpec(memory_space=pltpu.HBM)
    smoothed, norm = pl.pallas_call(
        functools.partial(kernel, L, R, S),
        name="smoother",
        out_shape=(
            jax.ShapeDtypeStruct((slab, nodes), f32),
            jax.ShapeDtypeStruct((1, slab), f32),
        ),
        in_specs=[hbm] * 7,
        out_specs=(hbm, vmem),
        scratch_shapes=[
            pltpu.VMEM((T, levels, CW), f32),
            pltpu.VMEM((S, half), f32),
            pltpu.VMEM((NB, (A + 1) * GROUP, BLOCK), f32),
            window(1), window(1), window(1), window(1), window(X - 1),
            pltpu.VMEM((X, NB, K, BLOCK), f32),
            pltpu.VMEM((X, NB, K, BLOCK), f32),
            pltpu.VMEM((levels, levels), f32),
            pltpu.VMEM((X, 2, K, BLOCK), f32),
            pltpu.VMEM((T, 2, slab, CW), f32),
            pltpu.VMEM((NB, BLOCK), f32),
            pltpu.VMEM((M, 1, BLOCK), f32),
            pltpu.VMEM((X, 1, BLOCK), f32),
            pltpu.VMEM((M, 1, BLOCK), f32),
            pltpu.VMEM((levels, levels), f32),
            pltpu.VMEM((levels, levels), f32),
            pltpu.VMEM((1, levels), f32),
            pltpu.SMEM(neighbors.shape, jnp.int32),
            dma((5,)), dma((T,)), dma(()),
            dma((T, R - 1)), dma((T, R)),
            *[dma((HC,)) for _ in range(8)],
            dma((X - 1, HC)), dma((X - 1, HC)),
            dma((T, X - 1)), dma((T, X)),
            dma((M - 1,)), dma((M,)), dma((X - 1,)), dma((X,)),
            dma((M - 1,)), dma((M,)),
            dma((T,)), dma((T,)), dma((T,)),
        ],
        compiler_params=pltpu.CompilerParams(
            collective_id=0, has_side_effects=True, vmem_limit_bytes=67043328
        ),
    )(
        source, weights, to_modes, from_modes, eigenvalue.reshape(1, levels),
        shifts.reshape(nodes // BLOCK, BLOCK), neighbors,
    )
    return smoothed, norm.reshape(slab)


def solution(mesh):
    return jax.shard_map(
        functools.partial(on_device, mesh.shape["lat"], mesh.shape["rad"]),
        mesh=mesh,
        in_specs=(P("rad", "lat"), P(), P(), P(), P("lat"), P(None, "lat"), P(None, "lat")),
        out_specs=(P("rad", "lat"), P("rad")),
        check_vma=False,
    )
```

time: 49.3 us -> 45.6 us (0.925)
  Pallas kernels: 46.1 us -> 42.4 us
    pallas_call x1, Pallas kernels: 46.1 us -> 42.4 us  [on_device(): pl.pallas_call(functools.partial(kernel, L, R, S), name='smoother', out_s...]
where the time goes in v3:
time: 45.6 us; the launch traced here: 45.5 us
  Pallas kernels  42.4 us (93%)
  local copies, waits for them, and re-layouts  2.39 us (5%)
  between operations  0.65 us (1%)
    pallas_call x1, Pallas kernels, on_device(): pl.pallas_call(functools.partial(kernel, L, R, S), name='smoother', out_s...  42.4 us
    unnamed x4, local copies, waits for them, and re-layouts  2.39 us

profile of v3, /device:TPU:0, one launch (start us, length us, event | category | flops | bytes accessed | tf_op | source)
XLA Modules:
  0.0 45.5 jit_solution(18040872630186476752)
XLA Ops:
  0.6 42.4 %smoother.1 = (f32[32,4096]{1,0:T(8,128)}, f32[1,32]{1,0:T(1,128)}) custom-call(f32[32,4096]{1,0:T(8,128)} %src.1, f32[31,4096]{1,0:T(8,128)} %w_hbm.1, f32[128,128]{1,0:T(8,128)} %to_hbm.1, f32[128,128]{1,0:T(8,128)} %from_hbm.1, f32[1,128]{1,0:T(1,128)} %bitcast.4, f32[32,128]{1,0:T(8,128)} %bitcast.3, s32[31,32]{1,0:T(8,128)} %nbr_hbm.1), custom_call_target="tpu_custom_call" | custom-call | tf_op jit(solution)/shard_map/smoother/pallas_call | solution.py:459
  43.1 0.0 copy-start
  43.1 1.9 %copy.11 = f32[32,4096]{1,0:T(8,128)} copy(f32[32,4096]{1,0:T(8,128)} %get-tuple-element.8) | data formatting | bytes 1048576
  45.0 0.0 copy-done
  45.0 0.5 %copy.12 = f32[32]{0:T(128)} copy(f32[32]{0:T(128)S(1)} %bitcast.5) | data formatting | bytes 256
Async XLA Ops:
  43.1 1.9 %copy-start = (f32[1,32]{1,0:T(1,128)S(1)}, f32[1,32]{1,0:T(1,128)}, u32[]{:S(2)}) copy-start(f32[1,32]{1,0:T(1,128)} %get-tuple-element.5) | copy-start | bytes 388

commit v4 on v3

--- a/solution.py
+++ b/solution.py
@@ -24,7 +24,7 @@
     L, R, S,
     src, w_hbm, to_hbm, from_hbm, eig_hbm, shift_hbm, nbr_hbm,
     out, res_ref,
-    gathered, wv, wr, outer1, inner1, outer2, inner2, others, modal, image, eig_t, coef, part,
+    gathered, wv, wr, outer1, inner1, outer2, inner2, others, modal, image, twice, eig_t, coef, part,
     rows, s1, s2, s3, to_ref, from_ref, eig_ref, nbr_ref,
     in_sem, own_sem, w_sem, ag_send, ag_recv,
     o1_send, o1_recv, i1_send, i1_recv, o2_send, o2_recv, i2_send, i2_recv, x_send, x_recv,
@@ -322,13 +322,6 @@
     plane_send(s1, s1_send, s1_recv)
     project_others(T - 1)
 
-    s2[chip] = plane_sum(s1, s1_send, s1_recv)
-    for j in range(1, X):
-        x = lax.rem(chip + j, X)
-        remote(
-            s2.at[chip], s2.at[chip], s2_send.at[j - 1], s2_recv.at[chip], lat, x * CORES + core
-        )
-
     inside = (NB // 2) * (1 - core)
     for j in range(1, X):
         x = lax.rem(chip + j, X)
@@ -344,23 +337,6 @@
             return carry
 
         lax.fori_loop(inside, inside + NB // 2, others_pass, 0)
-
-    for j in range(1, X):
-        x = lax.rem(chip + j, X)
-        arrived(s2.at[x], s2_send.at[j - 1], s2_recv.at[x])
-    for x in range(X):
-        column = jnp.transpose(jnp.broadcast_to(s2[x], (BLOCK, BLOCK)))
-        base, power = column[0:K], column[K:2 * K]
-        upper = 1.5 * jnp.sqrt(power / (base + 1e-06))
-        lower = upper * 0.125
-        center = (upper + lower) * 0.5
-        half_width = (upper - lower) * 0.5
-        sigma = center / half_width
-        rho_zero = 1.0 / sigma
-        rho_one = 1.0 / (2.0 * sigma - rho_zero)
-        second = 2.0 * rho_one / half_width
-        coef[x, 0] = (1.0 + rho_one * rho_zero) / center + second
-        coef[x, 1] = -second / center
 
     mine = jnp.concatenate(
         [
@@ -398,10 +374,8 @@
 
     def second_pass(buf, at):
         def step(b, carry):
-            field = image[chip, b]
-            value = operate(buf, at, chip, b, field)
-            final = modal[chip, b] - (coef[chip, 0] * field + coef[chip, 1] * value)
-            return carry + final * final
+            twice[b] = operate(buf, at, chip, b, image[chip, b])
+            return carry
 
         return step
 
@@ -409,21 +383,48 @@
         spread_at([(outer2, o_at + b), (inner2, i_at + b)], image[chip, b])
         return carry
 
+    def residual(b, carry):
+        final = modal[chip, b] - (coef[chip, 0] * image[chip, b] + coef[chip, 1] * twice[b])
+        return carry + final * final
+
     lax.fori_loop(0, NB, spread_own, 0)
     inner_wait(inner2, 0, i2_send, i2_recv)
     spread_halo(inner2, 0, inner_halo)
-    squares = lax.fori_loop(inside, inside + NB // 2, second_pass(inner2, i_at), zero)
-    for t in range(T // 2, T):
-        finish(t)
-    finish(0)
-
+    s2[chip] = plane_sum(s1, s1_send, s1_recv)
+    for j in range(1, X):
+        x = lax.rem(chip + j, X)
+        remote(
+            s2.at[chip], s2.at[chip], s2_send.at[j - 1], s2_recv.at[chip], lat, x * CORES + core
+        )
+
+    lax.fori_loop(inside, inside + NB // 2, second_pass(inner2, i_at), 0)
     outer_wait(outer2, o2_send, o2_recv)
     spread_halo(outer2, 0, outer_halo)
     outside = (NB // 2) * core
-    squares = lax.fori_loop(outside, outside + NB // 2, second_pass(outer2, o_at), squares)
-    s3[me] = lanes(squares)
+    lax.fori_loop(outside, outside + NB // 2, second_pass(outer2, o_at), 0)
+
+    for j in range(1, X):
+        x = lax.rem(chip + j, X)
+        arrived(s2.at[x], s2_send.at[j - 1], s2_recv.at[x])
+    for x in range(X):
+        column = jnp.transpose(jnp.broadcast_to(s2[x], (BLOCK, BLOCK)))
+        base, power = column[0:K], column[K:2 * K]
+        upper = 1.5 * jnp.sqrt(power / (base + 1e-06))
+        lower = upper * 0.125
+        center = (upper + lower) * 0.5
+        half_width = (upper - lower) * 0.5
+        sigma = center / half_width
+        rho_zero = 1.0 / sigma
+        rho_one = 1.0 / (2.0 * sigma - rho_zero)
+        second = 2.0 * rho_one / half_width
+        coef[x, 0] = (1.0 + rho_one * rho_zero) / center + second
+        coef[x, 1] = -second / center
+
+    s3[me] = lanes(lax.fori_loop(0, NB, residual, zero))
     plane_send(s3, s3_send, s3_recv)
-    for t in range(1, T // 2):
+    for t in range(T // 2, T):
+        finish(t)
+    for t in range(T // 2):
         finish(t)
 
     norm = jnp.sqrt(plane_sum(s3, s3_send, s3_recv) / (s2[chip] + 1e-06))
@@ -472,6 +473,7 @@
             window(1), window(1), window(1), window(1), window(X - 1),
             pltpu.VMEM((X, NB, K, BLOCK), f32),
             pltpu.VMEM((X, NB, K, BLOCK), f32),
+            pltpu.VMEM((NB, K, BLOCK), f32),
             pltpu.VMEM((levels, levels), f32),
             pltpu.VMEM((X, 2, K, BLOCK), f32),
             pltpu.VMEM((T, 2, slab, CW), f32),

time: 45.6 us -> 41.7 us (0.914)
  Pallas kernels: 42.4 us -> 38.5 us
    pallas_call x1, Pallas kernels: 42.4 us -> 38.5 us  [on_device(): pl.pallas_call(functools.partial(kernel, L, R, S), name='smoother', out_s...]
where the time goes in v4:
time: 41.7 us; the launch traced here: 41.5 us
  Pallas kernels  38.5 us (92%)
  local copies, waits for them, and re-layouts  2.39 us (6%)
  between operations  0.65 us (2%)
    pallas_call x1, Pallas kernels, on_device(): pl.pallas_call(functools.partial(kernel, L, R, S), name='smoother', out_s...  38.5 us
    unnamed x4, local copies, waits for them, and re-layouts  2.39 us

profile of v4, /device:TPU:0, one launch (start us, length us, event | category | flops | bytes accessed | tf_op | source)
XLA Modules:
  0.0 41.5 jit_solution(5897461086454019212)
XLA Ops:
  0.6 38.5 %smoother.1 = (f32[32,4096]{1,0:T(8,128)}, f32[1,32]{1,0:T(1,128)}) custom-call(f32[32,4096]{1,0:T(8,128)} %src.1, f32[31,4096]{1,0:T(8,128)} %w_hbm.1, f32[128,128]{1,0:T(8,128)} %to_hbm.1, f32[128,128]{1,0:T(8,128)} %from_hbm.1, f32[1,128]{1,0:T(1,128)} %bitcast.4, f32[32,128]{1,0:T(8,128)} %bitcast.3, s32[31,32]{1,0:T(8,128)} %nbr_hbm.1), custom_call_target="tpu_custom_call" | custom-call | tf_op jit(solution)/shard_map/smoother/pallas_call | solution.py:460
  39.2 0.0 copy-start
  39.2 1.9 %copy.11 = f32[32,4096]{1,0:T(8,128)} copy(f32[32,4096]{1,0:T(8,128)} %get-tuple-element.8) | data formatting | bytes 1048576
  41.0 0.0 copy-done
  41.0 0.5 %copy.12 = f32[32]{0:T(128)} copy(f32[32]{0:T(128)S(1)} %bitcast.5) | data formatting | bytes 256
Async XLA Ops:
  39.2 1.9 %copy-start = (f32[1,32]{1,0:T(1,128)S(1)}, f32[1,32]{1,0:T(1,128)}, u32[]{:S(2)}) copy-start(f32[1,32]{1,0:T(1,128)} %get-tuple-element.5) | copy-start | bytes 388
